TPU v7x, 512 devices: a whole 4x8x8 slice. The times are simulated.
512 devices in a mesh: dp: 4 (over x), expert: 128 (over z, y, core).
Axes of the slice: x: 4, y: 8, z: 8, core: 2. Of those that a mesh axis runs over, the one named last changes fastest.
Arguments:
- tokens: bfloat16 [8192, 2048], P(('dp', 'expert')), may hold values from -6 to 6
- cotangent: bfloat16 [8192, 2048], P(('dp', 'expert')), may hold values from -6 to 6
- routes: int32 [8192, 8], P(('dp', 'expert')), may hold values from 0 to 127, all different within a row; in each aligned block of 16 rows (0 to 15, 16 to 31, ...) at most 2 rows name the same one
- gate_values: float32 [8192, 8], P(('dp', 'expert')), may hold values from 0.1 to 1
- gate_weight: bfloat16 [128, 768, 2048], P('expert', 'dp'), may hold values from -0.125 to 0.125
- up_weight: bfloat16 [128, 768, 2048], P('expert', 'dp'), may hold values from -0.125 to 0.125
- down_weight: bfloat16 [128, 768, 2048], P('expert', None, 'dp'), may hold values from -0.21875 to 0.21875
Outputs:
- mixed: bfloat16 [8192, 2048], P(('dp', 'expert'))
- grad_gate_weight: bfloat16 [128, 768, 2048], P('expert', 'dp')
- grad_up_weight: bfloat16 [128, 768, 2048], P('expert', 'dp')
- grad_down_weight: bfloat16 [128, 768, 2048], P('expert', None, 'dp')
Inputs may be any that keep to these rules, and one draw needn't show every extreme that they name: `routes`: each row names 8 different experts. Among the rows of one device no expert is named more than 2 times, and in some device's rows some expert is named exactly 2 times.
All inputs are finite; a program needn't handle non-finite values.
Results may differ from a plain program's by a relative error of at most 0.0058.
Values may be sent and summed in bfloat16 or wider, within the bound.
A program may use at most 64 MiB of HBM per device.

v0:
```python
import jax
import jax.numpy as jnp
from jax import lax
from jax.sharding import PartitionSpec as P


def placement(routes, gate_values, experts, capacity):
    onehot = routes[:, :, None] == jnp.arange(experts, dtype=jnp.int32)[None, None, :]
    named = jnp.sum(onehot.astype(jnp.int32), axis=1)
    earlier = jnp.cumsum(named, axis=0) - named
    slot_ids = jnp.arange(capacity, dtype=jnp.int32)[None, :, None]
    placer = (named.T[:, None, :] == 1) & (earlier.T[:, None, :] == slot_ids)
    token_gate = jnp.sum(
        jnp.where(onehot, gate_values[:, :, None], jnp.zeros((), jnp.float32)), axis=1
    )
    slot_gate = jnp.sum(placer.astype(jnp.float32) * token_gate.T[:, None, :], axis=2)
    return (placer, slot_gate)


def body(tokens, cotangent, routes, gate_values, gate_weight, up_weight, down_weight):
    tok_rows = tokens.shape[0]
    width = tokens.shape[1]
    top_count = routes.shape[1]
    experts = lax.axis_size("expert")
    groups = lax.axis_size("dp")
    quarter = width // groups
    capacity = min(tok_rows, max(2, 2 * tok_rows * top_count // experts))
    placer, _ = placement(routes, gate_values, experts, capacity)
    row_input = jnp.einsum(
        "est,td->esd", placer.astype(jnp.bfloat16), tokens, preferred_element_type=jnp.float32
    ).astype(jnp.bfloat16)
    arrived_input = lax.all_to_all(row_input, "expert", split_axis=0, concat_axis=0, tiled=True)
    inputs_all = lax.all_gather(
        arrived_input.reshape(experts * capacity, width), "dp", axis=0, tiled=True
    )
    packed = jnp.concatenate(
        [cotangent.astype(jnp.float32), routes.astype(jnp.float32), gate_values], axis=1
    )
    col = lax.all_gather(packed, "dp", axis=0, tiled=False)
    col_routes = col[:, :, width : width + top_count].astype(jnp.int32)
    col_gates = col[:, :, width + top_count :]
    me = lax.axis_index("dp")
    cot_q = lax.dynamic_slice_in_dim(col[:, :, :width], me * quarter, quarter, axis=2).astype(
        jnp.bfloat16
    )
    col_placer, col_slot_gate = jax.vmap(lambda r, g: placement(r, g, experts, capacity))(
        col_routes, col_gates
    )
    picked_cot = jnp.einsum(
        "gest,gtd->egsd", col_placer.astype(jnp.bfloat16), cot_q, preferred_element_type=jnp.float32
    )
    row_cot = (jnp.transpose(col_slot_gate, (1, 0, 2))[:, :, :, None] * picked_cot).astype(
        jnp.bfloat16
    )
    arrived_cot = lax.all_to_all(row_cot, "expert", split_axis=0, concat_axis=0, tiled=True)
    cot_quarter = jnp.transpose(arrived_cot, (1, 0, 2, 3)).reshape(
        groups * experts * capacity, quarter
    )
    gate_local = gate_weight[0]
    up_local = up_weight[0]
    down_local = down_weight[0]
    contract_last = (((1,), (1,)), ((), ()))
    gate_pre = lax.dot_general(
        gate_local, inputs_all, contract_last, preferred_element_type=jnp.float32
    )
    up_pre = lax.dot_general(
        up_local, inputs_all, contract_last, preferred_element_type=jnp.float32
    )
    hidden_part = (jax.nn.silu(gate_pre) * up_pre).astype(jnp.bfloat16)
    hidden_all = lax.all_gather(hidden_part, "dp", axis=0, tiled=True)
    contract_lead = (((0,), (0,)), ((), ()))
    expert_out = lax.dot_general(
        hidden_all, down_local, contract_lead, preferred_element_type=jnp.float32
    ).astype(jnp.bfloat16)
    grad_down = jnp.dot(hidden_all, cot_quarter, preferred_element_type=jnp.float32).astype(
        jnp.bfloat16
    )
    grad_hidden = lax.psum_scatter(
        lax.dot_general(
            down_local, cot_quarter, contract_last, preferred_element_type=jnp.float32
        ).astype(jnp.bfloat16),
        "dp",
        scatter_dimension=0,
        tiled=True,
    ).astype(jnp.float32)
    sigma = jax.nn.sigmoid(gate_pre)
    grad_gate = (grad_hidden * up_pre * sigma * (1.0 + gate_pre * (1.0 - sigma))).astype(
        jnp.bfloat16
    )
    grad_up = (grad_hidden * jax.nn.silu(gate_pre)).astype(jnp.bfloat16)
    grad_gate_local = jnp.dot(grad_gate, inputs_all, preferred_element_type=jnp.float32).astype(
        jnp.bfloat16
    )
    grad_up_local = jnp.dot(grad_up, inputs_all, preferred_element_type=jnp.float32).astype(
        jnp.bfloat16
    )
    out_blocks = jnp.transpose(expert_out.reshape(groups, experts, capacity, quarter), (1, 0, 2, 3))
    returned = lax.all_to_all(out_blocks, "expert", split_axis=0, concat_axis=0, tiled=True)
    combine = col_placer.astype(jnp.float32) * col_slot_gate[:, :, :, None]
    mixed_q = jnp.einsum(
        "gest,egsd->gtd",
        combine,
        returned.astype(jnp.float32),
        precision=lax.Precision.HIGHEST,
        preferred_element_type=jnp.float32,
    ).astype(jnp.bfloat16)
    mixed = lax.all_to_all(mixed_q, "dp", split_axis=0, concat_axis=2, tiled=True)
    return (mixed[0], grad_gate_local[None], grad_up_local[None], grad_down[None])


def solution(mesh):
    in_specs = (
        P(("dp", "expert"), None),
        P(("dp", "expert"), None),
        P(("dp", "expert"), None),
        P(("dp", "expert"), None),
        P("expert", "dp", None),
        P("expert", "dp", None),
        P("expert", None, "dp"),
    )
    out_specs = (
        P(("dp", "expert"), None),
        P("expert", "dp", None),
        P("expert", "dp", None),
        P("expert", None, "dp"),
    )
    return jax.shard_map(body, mesh=mesh, in_specs=in_specs, out_specs=out_specs, check_vma=False)
```

profile of v0, /device:TPU:8, one launch (start us, length us, event | category | flops | bytes accessed | tf_op | source)
XLA Modules:
  0.0 215.8 jit_solution(4041124225692408910)
XLA Ops:
  7.2 0.0 copy-start
  7.2 0.0 all-gather.4.cloned.1.call-start
  7.2 0.8 copy.36
  8.0 0.1 convert_reduce_fusion.1
  8.2 1.3 convolution_convert_fusion
  9.5 1.1 copy.37
  10.6 48.6 %all_to_all.30 = bf16[128,2,2048]{2,1,0:T(2,128)(2,1)S(1)} all-to-all(bf16[128,2,2048]{2,1,0:T(2,128)(2,1)S(1)} %copy.37), channel_id=1, replica_groups=mesh['dp'=4,'expert'=128] {'expert'}, dimensions={0} | all-to-all | bytes 2097152 | tf_op jit(solution)/shard_map/all_to_all | solution.py:32
  59.2 1.2 reshape.30
  60.5 0.0 all-gather.4.cloned.1.call-update
  60.5 0.0 copy-done.4
  60.5 0.1 copy.34
  60.6 0.0 copy-done.5
  60.6 0.1 copy.35
  60.7 0.0 copy-done.3
  60.7 0.1 concatenate.3
  60.7 14.5 %all-gather = f32[64,2064]{1,0:T(8,128)S(1)} all-gather(f32[16,2064]{1,0:T(8,128)S(1)} %concatenate.3), channel_id=2, replica_groups=mesh['dp'=4,'expert'=128] {'dp'}, dimensions={0}, use_global_device_ids=true | all-gather | bytes 660480 | tf_op jit(solution)/shard_map/all_gather | solution.py:39
  75.3 0.1 slice_convert_fusion
  75.4 0.1 convert_reduce_fusion
  75.6 0.2 select_reduce_fusion
  75.9 0.5 fusion.2
  76.4 0.0 copy-start.8
  76.4 2.1 copy.41
  78.4 5.3 %all-to-all-start.3 = ((bf16[128,4,2,512]{3,2,1,0:T(2,128)(2,1)}), bf16[128,4,2,512]{3,2,1,0:T(2,128)(2,1)S(1)}, u32[]{:S(2)}, u32[]{:S(2)}) async-start(bf16[128,4,2,512]{3,2,1,0:T(2,128)(2,1)} %copy.41), calls=%async_computation.3 | async-start | bytes 2097152 | tf_op jit(solution)/shard_map/all_to_all | solution.py:55
  83.8 0.0 all-gather.6.cloned.1.call-start
  83.8 24.2 %all-gather.4.cloned.1.call-done = bf16[1024,2048]{1,0:T(8,128)(2,1)} async-done(((bf16[256,2048]{1,0:T(8,128)(2,1)}), bf16[1024,2048]{1,0:T(8,128)(2,1)}) %all-gather.4.cloned.1.call-update) | async-done | bytes 4194320 | tf_op jit(solution)/shard_map/all_gather | solution.py:33
  108.0 0.0 copy-done.8
  108.0 3.9 %convolution_bitcast_fusion.1 = f32[192,1024]{1,0:T(8,128)S(1)} fusion(bf16[1024,2048]{1,0:T(8,128)(2,1)} %all-gather.4.cloned.1.call-done, bf16[1,192,2048]{2,1,0:T(8,128)(2,1)S(1)} %copy-done.8), kind=kOutput, calls=%fused_computation.13 | convolution fusion | flops 805306368 | bytes 5767168 | tf_op jit(solution)/shard_map/dot_general | solution.py:63
  111.9 0.0 copy-done.6
  111.9 0.0 copy-start.10
  111.9 4.1 %multiply_convert_fusion = (bf16[192,1024]{1,0:T(8,128)(2,1)}, f32[192,1024]{1,0:T(8,128)}) fusion(f32[192,1024]{1,0:T(8,128)S(1)} %convolution_bitcast_fusion.1, bf16[1024,2048]{1,0:T(8,128)(2,1)S(1)} %copy-done.6, bf16[1,192,2048]{2,1,0:T(8,128)(2,1)} %param.12), kind=kOutput, calls=%fused_computation.28 | convolution fusion | flops 806486016 | bytes 6946816 | tf_op jit(solution)/shard_map/dot_general | solution.py:66
  116.0 0.0 copy-done.10
  116.0 0.0 all-gather.6.cloned.1.call-update
  116.0 0.2 reduce-scatter.2.cloned.1.call-start
  116.3 0.0 all-to-all-done.3
  116.3 0.7 copy.42
  117.0 0.4 reshape.32
  117.5 0.0 copy-done
  117.5 0.0 copy-start.1
  117.5 2.2 %fusion.3 = bf16[768,1024]{1,0:T(8,128)(2,1)} fusion(bf16[1024,512]{1,0:T(8,128)(2,1)S(1)} %reshape.32, bf16[1,768,512]{2,1,0:T(8,128)(2,1)S(1)} %copy-done), kind=kOutput, calls=%fused_computation.9 | convolution fusion | flops 806092800 | bytes 3407872 | tf_op jit(solution)/shard_map/dot_general | solution.py:79
  119.7 0.0 copy-done.1
  119.7 0.0 reduce-scatter.2.cloned.1.call-update
  119.7 28.1 %all-gather.6.cloned.1.call-done = bf16[768,1024]{1,0:T(8,128)(2,1)} async-done(((bf16[192,1024]{1,0:T(8,128)(2,1)}), bf16[768,1024]{1,0:T(8,128)(2,1)}) %all-gather.6.cloned.1.call-update) | async-done | bytes 1572880 | tf_op jit(solution)/shard_map/all_gather | solution.py:70
  147.8 2.4 %convolution_convert_fusion.4 = bf16[1024,512]{1,0:T(8,128)(2,1)S(1)} fusion(bf16[768,1024]{1,0:T(8,128)(2,1)} %all-gather.6.cloned.1.call-done, bf16[1,768,512]{2,1,0:T(8,128)(2,1)S(1)} %copy-done), kind=kOutput, calls=%fused_computation.8 | convolution fusion | flops 805830656 | bytes 3407872 | tf_op jit(solution)/shard_map/dot_general | solution.py:72
  150.2 0.4 reshape.31
  150.6 0.0 copy-start.11
  150.6 1.8 copy.51
  152.4 14.2 %all-to-all-start.1 = ((bf16[128,4,2,512]{3,2,1,0:T(2,128)(2,1)}), bf16[128,4,2,512]{3,2,1,0:T(2,128)(2,1)S(1)}, u32[]{:S(2)}, u32[]{:S(2)}) async-start(bf16[128,4,2,512]{3,2,1,0:T(2,128)(2,1)} %bitcast.70), calls=%async_computation.1 | async-start | bytes 2097152 | tf_op jit(solution)/shard_map/all_to_all | solution.py:98
  166.6 15.2 %reduce-scatter.2.cloned.1.call-done = bf16[192,1024]{1,0:T(8,128)(2,1)} async-done(((bf16[768,1024]{1,0:T(8,128)(2,1)}), bf16[192,1024]{1,0:T(8,128)(2,1)}) %reduce-scatter.2.cloned.1.call-update) | async-done | bytes 393232 | tf_op jit(solution)/shard_map/reduce_scatter | solution.py:78
  181.8 0.0 copy-done.11
  181.8 0.0 copy-start.13
  181.8 4.4 %fusion.1 = bf16[1,192,2048]{2,1,0:T(8,128)(2,1)} fusion(bf16[1024,2048]{1,0:T(8,128)(2,1)} %all-gather.4.cloned.1.call-done, bf16[192,1024]{1,0:T(8,128)(2,1)} %reduce-scatter.2.cloned.1.call-done, f32[192,1024]{1,0:T(8,128)S(1)} %copy-done.11), kind=kOutput, calls=%fused_computation.4 | convolution fusion | flops 807075840 | bytes 6160384 | tf_op jit(solution)/shard_map/dot_general | solution.py:94
  186.2 0.0 copy-done.7
  186.2 0.0 copy-done.12
  186.2 0.0 copy-done.13
  186.2 0.0 copy-start.2
  186.2 2.0 fusion
  188.3 9.8 %all-to-all-done.1 = bf16[128,4,2,512]{3,2,1,0:T(2,128)(2,1)S(1)} async-done(((bf16[128,4,2,512]{3,2,1,0:T(2,128)(2,1)}), bf16[128,4,2,512]{3,2,1,0:T(2,128)(2,1)S(1)}, u32[]{:S(2)}, u32[]{:S(2)}) %all-to-all-start.1) | async-done | bytes 1048608 | tf_op jit(solution)/shard_map/all_to_all | solution.py:98
  198.0 1.6 fusion.5
  199.7 3.3 %all-to-all-start.2 = ((bf16[4,16,512]{2,1,0:T(8,128)(2,1)}), bf16[4,16,512]{2,1,0:T(8,128)(2,1)S(1)}, u32[]{:S(2)}, u32[]{:S(2)}) async-start(bf16[4,16,512]{2,1,0:T(8,128)(2,1)} %fusion.5), calls=%async_computation.2 | async-start | bytes 131072 | tf_op jit(solution)/shard_map/all_to_all | solution.py:107
  203.0 0.0 copy-done.2
  203.0 3.3 %fusion.4 = bf16[1,768,512]{2,1,0:T(8,128)(2,1)} fusion(bf16[768,1024]{1,0:T(8,128)(2,1)} %all-gather.6.cloned.1.call-done, bf16[1024,512]{1,0:T(8,128)(2,1)S(1)} %copy-done.2), kind=kOutput, calls=%fused_computation.11 | convolution fusion | flops 805699584 | bytes 3407872 | tf_op jit(solution)/shard_map/dot_general | solution.py:75
  206.3 2.3 %all-to-all-done.2 = bf16[4,16,512]{2,1,0:T(8,128)(2,1)S(1)} async-done(((bf16[4,16,512]{2,1,0:T(8,128)(2,1)}), bf16[4,16,512]{2,1,0:T(8,128)(2,1)S(1)}, u32[]{:S(2)}, u32[]{:S(2)}) %all-to-all-start.2) | async-done | bytes 65568 | tf_op jit(solution)/shard_map/all_to_all | solution.py:107
  208.6 0.1 copy.40
  208.6 0.6 copy.47
  (17 shorter events, 0.2 us)
Async XLA Ops:
  7.2 110.3 %copy-start = (bf16[1,768,512]{2,1,0:T(8,128)(2,1)S(1)}, bf16[1,768,512]{2,1,0:T(8,128)(2,1)}, u32[]{:S(2)}) copy-start(bf16[1,768,512]{2,1,0:T(8,128)(2,1)} %param.13) | copy-start | bytes 2359300
  7.2 100.8 %all-gather.4.cloned.1.call-start = ((), (), s32[]{:S(2)}) async-start(), calls=%async_computation.5 | async-start | bytes 5242880 | tf_op jit(solution)/shard_map/all_gather | solution.py:33
  59.2 1.3 copy-start.4
  59.2 1.3 copy-start.5
  59.2 1.4 copy-start.3
  76.4 31.7 %copy-start.8 = (bf16[1,192,2048]{2,1,0:T(8,128)(2,1)S(1)}, bf16[1,192,2048]{2,1,0:T(8,128)(2,1)}, u32[]{:S(2)}) copy-start(bf16[1,192,2048]{2,1,0:T(8,128)(2,1)} %param.11) | copy-start | bytes 2359300
  78.4 37.8 %all-to-all-start.3 = ((bf16[128,4,2,512]{3,2,1,0:T(2,128)(2,1)}), bf16[128,4,2,512]{3,2,1,0:T(2,128)(2,1)S(1)}, u32[]{:S(2)}, u32[]{:S(2)}) async-start(bf16[128,4,2,512]{3,2,1,0:T(2,128)(2,1)} %copy.41), calls=%async_computation.3 | async-start | bytes 2097152 | tf_op jit(solution)/shard_map/all_to_all | solution.py:55
  83.8 64.0 %all-gather.6.cloned.1.call-start = ((), (), s32[]{:S(2)}) async-start(), calls=%async_computation.6 | async-start | bytes 1966080 | tf_op jit(solution)/shard_map/all_gather | solution.py:70
  108.0 3.9 %copy-start.6 = (bf16[1024,2048]{1,0:T(8,128)(2,1)S(1)}, bf16[1024,2048]{1,0:T(8,128)(2,1)}, u32[]{:S(2)}) copy-start(bf16[1024,2048]{1,0:T(8,128)(2,1)} %all-gather.4.cloned.1.call-done) | copy-start | bytes 12582916
  111.9 4.1 %copy-start.10 = (f32[192,1024]{1,0:T(8,128)}, f32[192,1024]{1,0:T(8,128)S(1)}, u32[]{:S(2)}) copy-start(f32[192,1024]{1,0:T(8,128)S(1)} %convolution_bitcast_fusion.1) | copy-start | bytes 2359300
  116.0 65.7 %reduce-scatter.2.cloned.1.call-start = ((), (), s32[]{:S(2)}) async-start(), calls=%async_computation.7 | async-start | bytes 1966080 | tf_op jit(solution)/shard_map/reduce_scatter | solution.py:78
  117.5 2.2 %copy-start.1 = (bf16[1024,512]{1,0:T(8,128)(2,1)}, bf16[1024,512]{1,0:T(8,128)(2,1)S(1)}, u32[]{:S(2)}) copy-start(bf16[1024,512]{1,0:T(8,128)(2,1)S(1)} %reshape.32) | copy-start | bytes 3145732
  150.6 31.2 %copy-start.11 = (f32[192,1024]{1,0:T(8,128)S(1)}, f32[192,1024]{1,0:T(8,128)}, u32[]{:S(2)}) copy-start(f32[192,1024]{1,0:T(8,128)} %copy-done.10) | copy-start | bytes 2359300
  152.4 45.6 %all-to-all-start.1 = ((bf16[128,4,2,512]{3,2,1,0:T(2,128)(2,1)}), bf16[128,4,2,512]{3,2,1,0:T(2,128)(2,1)S(1)}, u32[]{:S(2)}, u32[]{:S(2)}) async-start(bf16[128,4,2,512]{3,2,1,0:T(2,128)(2,1)} %bitcast.70), calls=%async_computation.1 | async-start | bytes 2097152 | tf_op jit(solution)/shard_map/all_to_all | solution.py:98
  181.8 4.4 %copy-start.7 = (bf16[1024,2048]{1,0:T(8,128)(2,1)S(1)}, bf16[1024,2048]{1,0:T(8,128)(2,1)}, u32[]{:S(2)}) copy-start(bf16[1024,2048]{1,0:T(8,128)(2,1)} %all-gather.4.cloned.1.call-done) | copy-start | bytes 12582916
  181.8 4.4 %copy-start.9 = (bf16[192,1024]{1,0:T(8,128)(2,1)S(1)}, bf16[192,1024]{1,0:T(8,128)(2,1)}, u32[]{:S(2)}) copy-start(bf16[192,1024]{1,0:T(8,128)(2,1)} %reduce-scatter.2.cloned.1.call-done) | copy-start | bytes 1179652
  181.8 4.4 %copy-start.12 = (f32[192,1024]{1,0:T(8,128)S(1)}, f32[192,1024]{1,0:T(8,128)}, u32[]{:S(2)}) copy-start(f32[192,1024]{1,0:T(8,128)} %copy-done.10) | copy-start | bytes 2359300
  181.8 4.4 %copy-start.13 = (f32[192,1024]{1,0:T(8,128)S(1)}, f32[192,1024]{1,0:T(8,128)}, u32[]{:S(2)}) copy-start(f32[192,1024]{1,0:T(8,128)} %get-tuple-element.7) | copy-start | bytes 2359300
  186.2 16.8 %copy-start.2 = (bf16[1024,512]{1,0:T(8,128)(2,1)S(1)}, bf16[1024,512]{1,0:T(8,128)(2,1)}, u32[]{:S(2)}) copy-start(bf16[1024,512]{1,0:T(8,128)(2,1)} %copy-done.1) | copy-start | bytes 3145732
  199.7 8.9 %all-to-all-start.2 = ((bf16[4,16,512]{2,1,0:T(8,128)(2,1)}), bf16[4,16,512]{2,1,0:T(8,128)(2,1)S(1)}, u32[]{:S(2)}, u32[]{:S(2)}) async-start(bf16[4,16,512]{2,1,0:T(8,128)(2,1)} %fusion.5), calls=%async_computation.2 | async-start | bytes 131072 | tf_op jit(solution)/shard_map/all_to_all | solution.py:107
Sparse Core Ops, SparseCore 0:
  60.6 47.3 all-gather.3
  116.2 31.5 all-gather.5
  150.6 31.1 reduce-scatter.1
where the time goes:
time: 216 us
  waiting for transfers between devices  79.6 us (37%)
  blocking collectives  63.1 us (29%)
  matrix products  25.7 us (12%)
  starting transfers between devices  23.1 us (11%)
  between operations  14 us (6%)
  local copies, waits for them, and re-layouts  9.6 us (4%)
    all_to_all x1, blocking collectives, body(): lax.all_to_all(row_input, 'expert', split_axis=0, concat_axis=0, tiled=True)  48.6 us
    all_gather x1, waiting for transfers between devices, body(): hidden_all = lax.all_gather(hidden_part, 'dp', axis=0, tiled=True)  28.1 us
    all_gather x1, waiting for transfers between devices, body(): lax.all_gather(arrived_input.reshape(experts * capacity, width), 'dp', ax...  24.2 us
    reduce_scatter x1, waiting for transfers between devices, body(): lax.psum_scatter(lax.dot_general(down_local, cot_quarter, contract_last,...  15.2 us
    all_gather x1, blocking collectives, body(): col = lax.all_gather(packed, 'dp', axis=0, tiled=False)  14.5 us
    all_to_all x1, starting transfers between devices, body(): lax.all_to_all(out_blocks, 'expert', split_axis=0, concat_axis=0, tiled=T...  14.2 us
    all_to_all x1, waiting for transfers between devices, body(): lax.all_to_all(out_blocks, 'expert', split_axis=0, concat_axis=0, tiled=T...  9.77 us
    all_to_all x1, starting transfers between devices, body(): lax.all_to_all(row_cot, 'expert', split_axis=0, concat_axis=0, tiled=True)  5.32 us
  transfers between devices with their start and end apart: 6, of which 5 were waited for; matrix products, arithmetic and copies ran while one was open for 13% of the time, Pallas kernels for 0%

commit v1 on v0

--- a/solution.py
+++ b/solution.py
@@ -67,7 +67,22 @@
         up_local, inputs_all, contract_last, preferred_element_type=jnp.float32
     )
     hidden_part = (jax.nn.silu(gate_pre) * up_pre).astype(jnp.bfloat16)
-    hidden_all = lax.all_gather(hidden_part, "dp", axis=0, tiled=True)
+    ways, here, step = (lax.axis_size("dp"), lax.axis_index("dp"), hidden_part.shape[0])
+    shape = [n * ways if d == 0 else n for d, n in enumerate(hidden_part.shape)]
+    hidden_all = lax.dynamic_update_slice_in_dim(
+        jnp.zeros(shape, hidden_part.dtype), hidden_part, here * step, axis=0
+    )
+    going_up = going_down = hidden_part
+    for far in range(1, ways // 2 + 1):
+        going_up = lax.ppermute(going_up, "dp", [(d, (d + 1) % ways) for d in range(ways)])
+        hidden_all = lax.dynamic_update_slice_in_dim(
+            hidden_all, going_up, (here - far) % ways * step, axis=0
+        )
+        if 2 * far < ways:
+            going_down = lax.ppermute(going_down, "dp", [(d, (d - 1) % ways) for d in range(ways)])
+            hidden_all = lax.dynamic_update_slice_in_dim(
+                hidden_all, going_down, (here + far) % ways * step, axis=0
+            )
     contract_lead = (((0,), (0,)), ((), ()))
     expert_out = lax.dot_general(
         hidden_all, down_local, contract_lead, preferred_element_type=jnp.float32

time: 216 us -> 225 us (1.042)
  local copies, waits for them, and re-layouts: 9.6 us -> 14.1 us
  waiting for transfers between devices: 79.6 us -> 83.7 us
    all_to_all x1, waiting for transfers between devices: 0.01 us -> 30.9 us  [body(): lax.all_to_all(row_cot, 'expert', split_axis=0, concat_axis=0, tiled=True)]
    all_gather x1 -> x0, waiting for transfers between devices: 28.1 us -> none  [body(): hidden_all = lax.all_gather(hidden_part, 'dp', axis=0, tiled=True)]
    ppermute x0 -> x3, waiting for transfers between devices: none -> 25.5 us  [the longest x2 25.5 us: body(): lax.ppermute(going_up, 'dp', [(d, (d + 1) % ways) for d in range(ways)])]
    all_gather x1, waiting for transfers between devices: 24.2 us -> 0.02 us  [body(): lax.all_gather(arrived_input.reshape(experts * capacity, width), 'dp', ax...]
    reduce_scatter x1, waiting for transfers between devices: 15.2 us -> 0.02 us  [body(): lax.psum_scatter(lax.dot_general(down_local, cot_quarter, contract_last,...]
    all_to_all x1, waiting for transfers between devices: 9.77 us -> 24.7 us  [body(): lax.all_to_all(out_blocks, 'expert', split_axis=0, concat_axis=0, tiled=T...]
    ppermute x0 -> x3, starting transfers between devices: none -> 9.13 us  [the longest x2 5.63 us: body(): lax.ppermute(going_up, 'dp', [(d, (d + 1) % ways) for d in range(ways)])]
    all_to_all x1, starting transfers between devices: 14.2 us -> 6.46 us  [body(): lax.all_to_all(out_blocks, 'expert', split_axis=0, concat_axis=0, tiled=T...]
  transfers between devices with their start and end apart: 6 -> 8, of which waited for: 5 -> 5; matrix products, arithmetic and copies ran while one was open for 13% -> 13% of each run, Pallas kernels for 0% -> 0%
where the time goes in v1:
time: 225 us; the launch traced here: 224 us
  waiting for transfers between devices  83.7 us (37%)
  blocking collectives  63.2 us (28%)
  starting transfers between devices  24.3 us (11%)
  matrix products  23.8 us (11%)
  between operations  14.4 us (6%)
  local copies, waits for them, and re-layouts  14.1 us (6%)
    all_to_all x1, blocking collectives, body(): lax.all_to_all(row_input, 'expert', split_axis=0, concat_axis=0, tiled=True)  48.6 us
    all_to_all x1, waiting for transfers between devices, body(): lax.all_to_all(row_cot, 'expert', split_axis=0, concat_axis=0, tiled=True)  30.9 us
    ppermute x2, waiting for transfers between devices, body(): lax.ppermute(going_up, 'dp', [(d, (d + 1) % ways) for d in range(ways)])  25.5 us
    all_to_all x1, waiting for transfers between devices, body(): lax.all_to_all(out_blocks, 'expert', split_axis=0, concat_axis=0, tiled=T...  24.7 us
    all_gather x1, blocking collectives, body(): col = lax.all_gather(packed, 'dp', axis=0, tiled=False)  14.5 us
    all_to_all x1, starting transfers between devices, body(): lax.all_to_all(out_blocks, 'expert', split_axis=0, concat_axis=0, tiled=T...  6.46 us
    ppermute x2, starting transfers between devices, body(): lax.ppermute(going_up, 'dp', [(d, (d + 1) % ways) for d in range(ways)])  5.63 us
    all_to_all x1, starting transfers between devices, body(): lax.all_to_all(row_cot, 'expert', split_axis=0, concat_axis=0, tiled=True)  5.32 us
  transfers between devices with their start and end apart: 8, of which 5 were waited for; matrix products, arithmetic and copies ran while one was open for 13% of the time, Pallas kernels for 0%

profile of v1, /device:TPU:8, one launch (start us, length us, event | category | flops | bytes accessed | tf_op | source)
XLA Modules:
  0.0 224.1 jit_solution(12196098250368525339)
XLA Ops:
  7.2 0.0 copy-start
  7.2 0.0 all-gather.3.cloned.1.call-start
  7.2 0.8 copy.36
  8.0 0.1 convert_reduce_fusion.1
  8.2 1.3 convolution_convert_fusion
  9.5 1.1 copy.37
  10.6 48.6 %all_to_all.30 = bf16[128,2,2048]{2,1,0:T(2,128)(2,1)S(1)} all-to-all(bf16[128,2,2048]{2,1,0:T(2,128)(2,1)S(1)} %copy.37), channel_id=1, replica_groups=mesh['dp'=4,'expert'=128] {'expert'}, dimensions={0} | all-to-all | bytes 2097152 | tf_op jit(solution)/shard_map/all_to_all | solution.py:32
  59.2 1.2 reshape.30
  60.5 0.0 all-gather.3.cloned.1.call-update
  60.5 0.0 copy-done.3
  60.5 0.1 copy.34
  60.6 0.0 copy-done.4
  60.6 0.1 copy.35
  60.7 0.0 copy-done.2
  60.7 0.1 concatenate.3
  60.7 14.5 %all-gather = f32[64,2064]{1,0:T(8,128)S(1)} all-gather(f32[16,2064]{1,0:T(8,128)S(1)} %concatenate.3), channel_id=2, replica_groups=mesh['dp'=4,'expert'=128] {'dp'}, dimensions={0}, use_global_device_ids=true | all-gather | bytes 660480 | tf_op jit(solution)/shard_map/all_gather | solution.py:39
  75.3 0.1 slice_convert_fusion
  75.4 0.1 convert_reduce_fusion
  75.6 0.2 select_reduce_fusion
  75.9 0.5 fusion.2
  76.4 2.1 copy.41
  78.4 5.3 %all-to-all-start.3 = ((bf16[128,4,2,512]{3,2,1,0:T(2,128)(2,1)}), bf16[128,4,2,512]{3,2,1,0:T(2,128)(2,1)S(1)}, u32[]{:S(2)}, u32[]{:S(2)}) async-start(bf16[128,4,2,512]{3,2,1,0:T(2,128)(2,1)} %copy.41), calls=%async_computation.3 | async-start | bytes 2097152 | tf_op jit(solution)/shard_map/all_to_all | solution.py:55
  83.8 0.0 reduce-scatter.2.cloned.1.call-start
  83.8 30.9 %all-to-all-done.3 = bf16[128,4,2,512]{3,2,1,0:T(2,128)(2,1)S(1)} async-done(((bf16[128,4,2,512]{3,2,1,0:T(2,128)(2,1)}), bf16[128,4,2,512]{3,2,1,0:T(2,128)(2,1)S(1)}, u32[]{:S(2)}, u32[]{:S(2)}) %all-to-all-start.3) | async-done | bytes 1048608 | tf_op jit(solution)/shard_map/all_to_all | solution.py:55
  114.7 0.7 copy.42
  115.4 0.4 reshape.32
  115.9 0.0 copy-done
  115.9 0.0 copy-start.1
  115.9 2.2 fusion.3
  118.1 0.0 reduce-scatter.2.cloned.1.call-update
  118.1 0.0 all-gather.3.cloned.1.call-done
  118.2 1.1 copy-done.7
  119.2 3.9 %convolution_bitcast_fusion.1 = f32[192,1024]{1,0:T(8,128)S(1)} fusion(bf16[1024,2048]{1,0:T(8,128)(2,1)} %all-gather.3.cloned.1.call-done, bf16[1,192,2048]{2,1,0:T(8,128)(2,1)S(1)} %copy-done.7), kind=kOutput, calls=%fused_computation.13 | convolution fusion | flops 805306368 | bytes 5767168 | tf_op jit(solution)/shard_map/dot_general | solution.py:63
  123.1 0.0 copy-start.10
  123.1 0.0 copy-start.8
  123.1 0.2 broadcast_in_dim.22
  123.3 0.0 copy-done.5
  123.3 1.2 copy-done.8
  124.5 2.6 %constant_dynamic-update-slice_fusion.3 = (bf16[768,1024]{1,0:T(8,128)(2,1)S(1)}, bf16[192,1024]{1,0:T(8,128)(2,1)}, f32[192,1024]{1,0:T(8,128)}) fusion(bf16[768,1024]{1,0:T(8,128)(2,1)S(1)} %broadcast_in_dim.22, s32[]{:T(128)S(6)} %select_n.35, f32[192,1024]{1,0:T(8,128)S(1)} %convolution_bitcast_fusion.1, bf16[1024,2048]{1,0:T(8,128)(2,1)S(1)} %copy-done.5, ...), kind=kOutput, calls=%fused_computation.63 | convolution fusion | flops 806486016 | bytes 7340036 | tf_op jit(solution)/shard_map/dot_general | solution.py:66
  127.1 0.0 copy-done.10
  127.1 3.5 %collective-permute-start = (bf16[192,1024]{1,0:T(8,128)(2,1)}, bf16[192,1024]{1,0:T(8,128)(2,1)S(1)}, u32[]{:S(2)}, u32[]{:S(2)}) collective-permute-start(bf16[192,1024]{1,0:T(8,128)(2,1)} %get-tuple-element.5), channel_id=1, source_target_pairs={{0,128},{128,256},{256,384},{384,0},{1,129},{129,257},{257,385},{3... | collective-permute-start | bytes 1179656 | tf_op jit(solution)/shard_map/ppermute | solution.py:77
  130.7 3.5 %collective-permute-start.1 = (bf16[192,1024]{1,0:T(8,128)(2,1)}, bf16[192,1024]{1,0:T(8,128)(2,1)}, u32[]{:S(2)}, u32[]{:S(2)}) collective-permute-start(bf16[192,1024]{1,0:T(8,128)(2,1)} %get-tuple-element.5), channel_id=1, source_target_pairs={{0,384},{128,0},{256,128},{384,256},{1,385},{129,1},{257,129},{385... | collective-permute-start | bytes 1179656 | tf_op jit(solution)/shard_map/ppermute | solution.py:82
  134.2 15.1 %collective-permute-done = bf16[192,1024]{1,0:T(8,128)(2,1)S(1)} collective-permute-done((bf16[192,1024]{1,0:T(8,128)(2,1)}, bf16[192,1024]{1,0:T(8,128)(2,1)S(1)}, u32[]{:S(2)}, u32[]{:S(2)}) %collective-permute-start) | collective-permute-done | bytes 393248 | tf_op jit(solution)/shard_map/ppermute | solution.py:77
  149.3 2.1 collective-permute-start.2
  151.5 0.0 collective-permute-done.1
  151.5 1.0 constant_dynamic-update-slice_fusion.1
  152.6 10.3 %collective-permute-done.2 = bf16[192,1024]{1,0:T(8,128)(2,1)S(1)} collective-permute-done((bf16[192,1024]{1,0:T(8,128)(2,1)S(1)}, bf16[192,1024]{1,0:T(8,128)(2,1)S(1)}, u32[]{:S(2)}, u32[]{:S(2)}) %collective-permute-start.2) | collective-permute-done | bytes 393248 | tf_op jit(solution)/shard_map/ppermute | solution.py:77
  163.0 2.0 convolution_convert_fusion.4
  165.0 1.5 reshape.31
  166.4 1.7 copy.51
  168.1 6.5 %all-to-all-start.1 = ((bf16[128,4,2,512]{3,2,1,0:T(2,128)(2,1)}), bf16[128,4,2,512]{3,2,1,0:T(2,128)(2,1)S(1)}, u32[]{:S(2)}, u32[]{:S(2)}) async-start(bf16[128,4,2,512]{3,2,1,0:T(2,128)(2,1)} %bitcast.70), calls=%async_computation.1 | async-start | bytes 2097152 | tf_op jit(solution)/shard_map/all_to_all | solution.py:113
  174.6 0.0 reduce-scatter.2.cloned.1.call-done
  174.6 0.0 copy-start.11
  174.7 0.0 copy-start.12
  174.7 4.6 %fusion.1 = bf16[1,192,2048]{2,1,0:T(8,128)(2,1)} fusion(bf16[1024,2048]{1,0:T(8,128)(2,1)} %all-gather.3.cloned.1.call-done, bf16[192,1024]{1,0:T(8,128)(2,1)} %reduce-scatter.2.cloned.1.call-done, f32[192,1024]{1,0:T(8,128)} %copy-done.10), kind=kOutput, calls=%fused_computation.4 | convolution fusion | flops 807075840 | bytes 6160384 | tf_op jit(solution)/shard_map/dot_general | solution.py:109
  179.3 0.0 copy-done.6
  179.3 2.0 fusion
  181.3 24.7 %all-to-all-done.1 = bf16[128,4,2,512]{3,2,1,0:T(2,128)(2,1)S(1)} async-done(((bf16[128,4,2,512]{3,2,1,0:T(2,128)(2,1)}), bf16[128,4,2,512]{3,2,1,0:T(2,128)(2,1)S(1)}, u32[]{:S(2)}, u32[]{:S(2)}) %all-to-all-start.1) | async-done | bytes 1048608 | tf_op jit(solution)/shard_map/all_to_all | solution.py:113
  206.1 1.6 fusion.5
  207.7 3.3 %all-to-all-start.2 = ((bf16[4,16,512]{2,1,0:T(8,128)(2,1)}), bf16[4,16,512]{2,1,0:T(8,128)(2,1)S(1)}, u32[]{:S(2)}, u32[]{:S(2)}) async-start(bf16[4,16,512]{2,1,0:T(8,128)(2,1)} %fusion.5), calls=%async_computation.2 | async-start | bytes 131072 | tf_op jit(solution)/shard_map/all_to_all | solution.py:122
  211.0 3.1 %fusion.4 = bf16[1,768,512]{2,1,0:T(8,128)(2,1)} fusion(bf16[768,1024]{1,0:T(8,128)(2,1)S(1)} %constant_dynamic-update-slice_fusion, bf16[1024,512]{1,0:T(8,128)(2,1)} %copy-done.1), kind=kOutput, calls=%fused_computation.11 | convolution fusion | flops 805699584 | bytes 3407872 | tf_op jit(solution)/shard_map/dot_general | solution.py:90
  214.1 2.5 %all-to-all-done.2 = bf16[4,16,512]{2,1,0:T(8,128)(2,1)S(1)} async-done(((bf16[4,16,512]{2,1,0:T(8,128)(2,1)}), bf16[4,16,512]{2,1,0:T(8,128)(2,1)S(1)}, u32[]{:S(2)}, u32[]{:S(2)}) %all-to-all-start.2) | async-done | bytes 65568 | tf_op jit(solution)/shard_map/all_to_all | solution.py:122
  216.6 0.1 copy.40
  216.6 0.6 copy.47
  (22 shorter events, 0.3 us)
Async XLA Ops:
  7.2 108.7 %copy-start = (bf16[1,768,512]{2,1,0:T(8,128)(2,1)S(1)}, bf16[1,768,512]{2,1,0:T(8,128)(2,1)}, u32[]{:S(2)}) copy-start(bf16[1,768,512]{2,1,0:T(8,128)(2,1)} %param.13) | copy-start | bytes 2359300
  7.2 111.0 %all-gather.3.cloned.1.call-start = ((), (), s32[]{:S(2)}) async-start(), calls=%async_computation.5 | async-start | bytes 5242880 | tf_op jit(solution)/shard_map/all_gather | solution.py:33
  59.2 1.2 copy-start.3
  59.2 1.3 copy-start.4
  59.2 1.4 copy-start.2
  78.4 36.3 %all-to-all-start.3 = ((bf16[128,4,2,512]{3,2,1,0:T(2,128)(2,1)}), bf16[128,4,2,512]{3,2,1,0:T(2,128)(2,1)S(1)}, u32[]{:S(2)}, u32[]{:S(2)}) async-start(bf16[128,4,2,512]{3,2,1,0:T(2,128)(2,1)} %copy.41), calls=%async_computation.3 | async-start | bytes 2097152 | tf_op jit(solution)/shard_map/all_to_all | solution.py:55
  83.8 90.8 %reduce-scatter.2.cloned.1.call-start = ((), (), s32[]{:S(2)}) async-start(), calls=%async_computation.6 | async-start | bytes 1966080 | tf_op jit(solution)/shard_map/reduce_scatter | solution.py:93
  115.9 2.2 copy-start.1
  118.1 1.1 copy-start.7
  119.2 4.1 %copy-start.5 = (bf16[1024,2048]{1,0:T(8,128)(2,1)S(1)}, bf16[1024,2048]{1,0:T(8,128)(2,1)}, u32[]{:S(2)}) copy-start(bf16[1024,2048]{1,0:T(8,128)(2,1)} %all-gather.3.cloned.1.call-done) | copy-start | bytes 12582916
  123.1 4.0 %copy-start.10 = (f32[192,1024]{1,0:T(8,128)}, f32[192,1024]{1,0:T(8,128)S(1)}, u32[]{:S(2)}) copy-start(f32[192,1024]{1,0:T(8,128)S(1)} %convolution_bitcast_fusion.1) | copy-start | bytes 2359300
  123.1 1.4 copy-start.8
  127.1 22.2 %collective-permute-start = (bf16[192,1024]{1,0:T(8,128)(2,1)}, bf16[192,1024]{1,0:T(8,128)(2,1)S(1)}, u32[]{:S(2)}, u32[]{:S(2)}) collective-permute-start(bf16[192,1024]{1,0:T(8,128)(2,1)} %get-tuple-element.5), channel_id=1, source_target_pairs={{0,128},{128,256},{256,384},{384,0},{1,129},{129,257},{257,385},{3... | collective-permute-start | bytes 1179656 | tf_op jit(solution)/shard_map/ppermute | solution.py:77
  130.7 20.9 %collective-permute-start.1 = (bf16[192,1024]{1,0:T(8,128)(2,1)}, bf16[192,1024]{1,0:T(8,128)(2,1)}, u32[]{:S(2)}, u32[]{:S(2)}) collective-permute-start(bf16[192,1024]{1,0:T(8,128)(2,1)} %get-tuple-element.5), channel_id=1, source_target_pairs={{0,384},{128,0},{256,128},{384,256},{1,385},{129,1},{257,129},{385... | collective-permute-start | bytes 1179656 | tf_op jit(solution)/shard_map/ppermute | solution.py:82
  149.3 13.6 %collective-permute-start.2 = (bf16[192,1024]{1,0:T(8,128)(2,1)S(1)}, bf16[192,1024]{1,0:T(8,128)(2,1)S(1)}, u32[]{:S(2)}, u32[]{:S(2)}) collective-permute-start(bf16[192,1024]{1,0:T(8,128)(2,1)S(1)} %collective-permute-done), channel_id=1, source_target_pairs={{0,128},{128,256},{256,384},{384,0},{1,129},{129,257},{257,385},{3... | collective-permute-start | bytes 1179656 | tf_op jit(solution)/shard_map/ppermute | solution.py:77
  168.1 37.9 %all-to-all-start.1 = ((bf16[128,4,2,512]{3,2,1,0:T(2,128)(2,1)}), bf16[128,4,2,512]{3,2,1,0:T(2,128)(2,1)S(1)}, u32[]{:S(2)}, u32[]{:S(2)}) async-start(bf16[128,4,2,512]{3,2,1,0:T(2,128)(2,1)} %bitcast.70), calls=%async_computation.1 | async-start | bytes 2097152 | tf_op jit(solution)/shard_map/all_to_all | solution.py:113
  174.6 4.7 %copy-start.6 = (bf16[1024,2048]{1,0:T(8,128)(2,1)S(1)}, bf16[1024,2048]{1,0:T(8,128)(2,1)}, u32[]{:S(2)}) copy-start(bf16[1024,2048]{1,0:T(8,128)(2,1)} %all-gather.3.cloned.1.call-done) | copy-start | bytes 12582916
  174.6 4.6 %copy-start.9 = (bf16[192,1024]{1,0:T(8,128)(2,1)S(1)}, bf16[192,1024]{1,0:T(8,128)(2,1)}, u32[]{:S(2)}) copy-start(bf16[192,1024]{1,0:T(8,128)(2,1)} %reduce-scatter.2.cloned.1.call-done) | copy-start | bytes 1179652
  174.6 4.6 %copy-start.11 = (f32[192,1024]{1,0:T(8,128)S(1)}, f32[192,1024]{1,0:T(8,128)}, u32[]{:S(2)}) copy-start(f32[192,1024]{1,0:T(8,128)} %copy-done.10) | copy-start | bytes 2359300
  174.7 4.6 %copy-start.12 = (f32[192,1024]{1,0:T(8,128)S(1)}, f32[192,1024]{1,0:T(8,128)}, u32[]{:S(2)}) copy-start(f32[192,1024]{1,0:T(8,128)} %get-tuple-element.8) | copy-start | bytes 2359300
  207.7 8.9 %all-to-all-start.2 = ((bf16[4,16,512]{2,1,0:T(8,128)(2,1)}), bf16[4,16,512]{2,1,0:T(8,128)(2,1)S(1)}, u32[]{:S(2)}, u32[]{:S(2)}) async-start(bf16[4,16,512]{2,1,0:T(8,128)(2,1)} %fusion.5), calls=%async_computation.2 | async-start | bytes 131072 | tf_op jit(solution)/shard_map/all_to_all | solution.py:122
Sparse Core Ops, SparseCore 0:
  60.6 47.3 all-gather.2
  118.2 31.6 reduce-scatter.1
